TPU v7x, 256 devices: a whole 4x4x8 slice. The times are simulated.
256 devices in a mesh: aux: 16 (over x, y), occ: 16 (over z, core).
Axes of the slice: x: 4, y: 4, z: 8, core: 2. Of those that a mesh axis runs over, the one named last changes fastest.
Arguments:
- integrals: bfloat16 [32, 384, 128, 128], P('aux', 'occ'), may hold values from -1.5 to 1.5
- coefficients: bfloat16 [4096, 384], P('occ'), may hold values from -0.21875 to 0.21875
- pair_rows: int32 [16, 384], P('aux', 'occ'), may hold values from 0 to 1
- pair_cols: int32 [16, 384], P('aux', 'occ'), may hold values from 0 to 31
- pair_count: int32 [16, 16], P('aux', 'occ'), may hold values from 1 to 24, as said below
- row_blocks: int32 [32], replicated, may hold values from 0 to 31, each once
Outputs:
- exchange_matrix: float32 [4096, 4096], P('aux', 'occ')
Inputs may be any that keep to these rules, and one draw needn't show every extreme that they name: `pair_count`: at most 24 live slots for each auxiliary block and row owner, and some auxiliary block and owner has exactly 24.
All inputs are finite; a program needn't handle non-finite values.
Results may differ from a plain program's by a relative error of at most 0.0022.
Values may be sent and summed in bfloat16 or wider, within the bound.
A program may use at most 64 MiB of HBM per device.

v0:
```python
import jax
import jax.numpy as jnp
from jax import lax
from jax.sharding import PartitionSpec as P


def contract_rows(first, second):
    return jnp.einsum("pni,pmi->nm", first, second, preferred_element_type=jnp.float32)


def local(integrals, coefficients, pair_rows, pair_cols, pair_count, row_blocks):
    aux_count, slots, block_size, _ = integrals.shape
    block_total = row_blocks.shape[0]
    occ_size = lax.axis_size("occ")
    own_blocks = block_total // occ_size
    strip_width = own_blocks * block_size
    full_coeff = lax.all_gather(coefficients, "occ", axis=0, tiled=True)
    orbitals = full_coeff.shape[1]
    coeff_blocks = full_coeff.reshape(block_total, block_size, orbitals)
    basis_block = row_blocks[pair_cols[0]]
    gathered = jnp.take(coeff_blocks, basis_block, axis=0)
    live = jnp.arange(slots, dtype=jnp.int32) < pair_count[0, 0]
    placing = (pair_rows[0][None, :] == jnp.arange(own_blocks, dtype=jnp.int32)[:, None]) & live[
        None, :
    ]
    weights = jnp.where(placing[:, :, None, None], gathered[None], jnp.zeros((), gathered.dtype))
    summed_half = jnp.einsum(
        "psmn,rsni->prmi", integrals, weights, preferred_element_type=jnp.float32
    )
    half = summed_half.reshape(aux_count, strip_width, orbitals).astype(jnp.bfloat16)
    strip = contract_rows(lax.all_gather(half, "occ", axis=1, tiled=True), half)
    return lax.psum_scatter(strip, "aux", scatter_dimension=0, tiled=True)


def solution(mesh):
    return jax.shard_map(
        local,
        mesh=mesh,
        in_specs=(
            P("aux", "occ", None, None),
            P("occ", None),
            P("aux", "occ"),
            P("aux", "occ"),
            P("aux", "occ"),
            P(),
        ),
        out_specs=P("aux", "occ"),
        check_vma=False,
    )
```

profile of v0, /device:TPU:2, one launch (start us, length us, event | category | flops | bytes accessed | tf_op | source)
XLA Modules:
  0.0 201.0 jit_solution(10329253605268713100)
XLA Ops:
  6.5 0.0 copy-start
  6.5 0.0 all-gather.3.cloned.1.call-start
  6.5 0.7 all-gather.3.cloned.1.call-update
  7.3 0.0 all-gather.5.cloned.1.call-start
  8.0 0.7 fusion.22
  8.6 1.4 gather_fusion
  10.0 0.7 compare_and_fusion.1
  10.7 42.5 %all-gather.3.cloned.1.call-done = bf16[4096,384]{1,0:T(8,128)(2,1)} async-done(((bf16[256,384]{1,0:T(8,128)(2,1)}), bf16[4096,384]{1,0:T(8,128)(2,1)}) %all-gather.3.cloned.1.call-update) | async-done | bytes 3145744 | tf_op jit(solution)/shard_map/all_gather | solution.py:17
  53.2 4.4 %gather_fusion.1 = bf16[24,128,384]{2,1,0:T(8,128)(2,1)} fusion(bf16[32,128,384]{2,1,0:T(8,128)(2,1)} %bitcast.48, s32[1024]{0:T(1024)S(1)} %pad_clamp_fusion), kind=kCustom, calls=%fused_computation.1 | custom fusion | bytes 4718688 | tf_op jit(solution)/shard_map/jit(_take)/gather | solution.py:21
  57.5 2.0 broadcast_select_fusion
  59.5 0.0 copy-done
  59.5 1.5 fusion.17
  61.0 0.8 copy.7
  61.8 0.0 all-gather.5.cloned.1.call-update
  61.8 0.0 reduce-scatter.2.cloned.1.call-start
  61.9 44.8 %all-gather.5.cloned.1.call-done = bf16[2,4096,384]{2,1,0:T(8,128)(2,1)} async-done(((bf16[2,256,384]{2,1,0:T(8,128)(2,1)}), bf16[2,4096,384]{2,1,0:T(8,128)(2,1)}) %all-gather.5.cloned.1.call-update) | async-done | bytes 6291472 | tf_op jit(solution)/shard_map/all_gather | solution.py:31
  106.7 6.7 %convolution_bitcast_fusion = f32[4096,256]{1,0:T(8,128)} fusion(bf16[2,4096,384]{2,1,0:T(8,128)(2,1)} %all-gather.5.cloned.1.call-done, bf16[2,256,384]{2,1,0:T(8,128)(2,1)} %bitcast.47), kind=kOutput, calls=%fused_computation.2 | convolution fusion | flops 1610612736 | bytes 10878976 | tf_op jit(solution)/shard_map/pni,pmi->nm/dot_general | solution.py:8
  113.3 0.0 reduce-scatter.2.cloned.1.call-update
  113.3 81.1 %reduce-scatter.2.cloned.1.call-done = f32[256,256]{1,0:T(8,128)} async-done(((f32[4096,256]{1,0:T(8,128)}), f32[256,256]{1,0:T(8,128)}) %reduce-scatter.2.cloned.1.call-update) | async-done | bytes 262160 | tf_op jit(solution)/shard_map/reduce_scatter | solution.py:32
  (5 shorter events, 0.0 us)
Async XLA Ops:
  6.5 53.0 %copy-start = (bf16[2,24,128,128]{3,2,1,0:T(8,128)(2,1)S(1)}, bf16[2,24,128,128]{3,2,1,0:T(8,128)(2,1)}, u32[]{:S(2)}) copy-start(bf16[2,24,128,128]{3,2,1,0:T(8,128)(2,1)} %param.6) | copy-start | bytes 4718596
  6.5 46.6 %all-gather.3.cloned.1.call-start = ((), (), s32[]{:S(2)}) async-start(), calls=%async_computation.1 | async-start | bytes 3342336 | tf_op jit(solution)/shard_map/all_gather | solution.py:17
  7.3 99.4 %all-gather.5.cloned.1.call-start = ((), (), s32[]{:S(2)}) async-start(), calls=%async_computation.2 | async-start | bytes 6684672 | tf_op jit(solution)/shard_map/all_gather | solution.py:31
  61.8 132.6 %reduce-scatter.2.cloned.1.call-start = ((), (), s32[]{:S(2)}) async-start(), calls=%async_computation.3 | async-start | bytes 4456448 | tf_op jit(solution)/shard_map/reduce_scatter | solution.py:32
Sparse Core Ops, SparseCore 0:
  9.2 43.9 all-gather.2
  62.0 44.6 all-gather.4
  113.5 80.9 reduce-scatter.1
where the time goes:
time: 201 us
  waiting for transfers between devices  169 us (84%)
  between operations  13.8 us (7%)
  matrix products  8.13 us (4%)
  local copies, waits for them, and re-layouts  6.52 us (3%)
  other arithmetic  3.35 us (2%)
    reduce_scatter x1, waiting for transfers between devices, local(): return lax.psum_scatter(strip, 'aux', scatter_dimension=0, tiled=True)  81.1 us
    all_gather x1, waiting for transfers between devices, local(): strip = contract_rows(lax.all_gather(half, 'occ', axis=1, tiled=True), half)  44.8 us
    all_gather x1, waiting for transfers between devices, local(): full_coeff = lax.all_gather(coefficients, 'occ', axis=0, tiled=True)  42.5 us
    dot_general x1, matrix products, contract_rows(): jnp.einsum('pni,pmi->nm', first, second, preferred_element_type=jnp.float32)  6.66 us
    gather x1, local copies, waits for them, and re-layouts, local(): gathered = jnp.take(coeff_blocks, basis_block, axis=0)  4.35 us
  transfers between devices with their start and end apart: 3, of which 3 were waited for; matrix products, arithmetic and copies ran while one was open for 1% of the time, Pallas kernels for 0%

commit v1 on v0

--- a/solution.py
+++ b/solution.py
@@ -28,7 +28,14 @@
         "psmn,rsni->prmi", integrals, weights, preferred_element_type=jnp.float32
     )
     half = summed_half.reshape(aux_count, strip_width, orbitals).astype(jnp.bfloat16)
-    strip = contract_rows(lax.all_gather(half, "occ", axis=1, tiled=True), half)
+
+    def detail_screen_all(base_x, a_name):
+        world_n = lax.axis_size(a_name)
+        grid = [world_n if b == 1 else 1 for b in range(base_x.ndim)]
+        m_next = jnp.tile(base_x, grid)
+        return lax.all_to_all(m_next, a_name, concat_axis=1, tiled=True, split_axis=1)
+
+    strip = contract_rows(detail_screen_all(half, "occ"), half)
     return lax.psum_scatter(strip, "aux", scatter_dimension=0, tiled=True)
 
 

time: 201 us -> 302 us (1.50)
  blocking collectives: 0 us -> 144 us
  waiting for transfers between devices: 169 us -> 124 us
  local copies, waits for them, and re-layouts: 6.52 us -> 11.2 us
    all_to_all x0 -> x1, blocking collectives: none -> 144 us  [detail_screen_all(): lax.all_to_all(m_next, a_name, concat_axis=1, tiled=True, split_axis=1)]
    all_gather x1 -> x0, waiting for transfers between devices: 44.8 us -> none  [local(): strip = contract_rows(lax.all_gather(half, 'occ', axis=1, tiled=True), half)]
    another operation x0 -> x1, local copies, waits for them, and re-layouts: none -> 5.06 us  [detail_screen_all(): m_next = jnp.tile(base_x, grid)]
  transfers between devices with their start and end apart: 3 -> 2, of which waited for: 3 -> 2; matrix products, arithmetic and copies ran while one was open for 1% -> 1% of each run, Pallas kernels for 0% -> 0%
where the time goes in v1:
time: 302 us
  blocking collectives  144 us (48%)
  waiting for transfers between devices  124 us (41%)
  between operations  14.1 us (5%)
  local copies, waits for them, and re-layouts  11.2 us (4%)
  matrix products  5.26 us (2%)
  other arithmetic  3.35 us (1%)
    all_to_all x1, blocking collectives, detail_screen_all(): lax.all_to_all(m_next, a_name, concat_axis=1, tiled=True, split_axis=1)  144 us
    reduce_scatter x1, waiting for transfers between devices, local(): return lax.psum_scatter(strip, 'aux', scatter_dimension=0, tiled=True)  80.9 us
    all_gather x1, waiting for transfers between devices, local(): full_coeff = lax.all_gather(coefficients, 'occ', axis=0, tiled=True)  42.5 us
  transfers between devices with their start and end apart: 2, of which 2 were waited for; matrix products, arithmetic and copies ran while one was open for 1% of the time, Pallas kernels for 0%

profile of v1, /device:TPU:2, one launch (start us, length us, event | category | flops | bytes accessed | tf_op | source)
XLA Modules:
  0.0 301.9 jit_solution(18211739926151828311)
XLA Ops:
  6.5 0.0 copy-start
  6.5 0.0 all-gather.2.cloned.1.call-start
  6.5 0.7 all-gather.2.cloned.1.call-update
  7.3 0.0 reduce-scatter.2.cloned.1.call-start
  8.0 0.7 fusion.27
  8.6 1.4 gather_fusion
  10.0 0.7 compare_and_fusion.1
  10.7 42.5 %all-gather.2.cloned.1.call-done = bf16[4096,384]{1,0:T(8,128)(2,1)} async-done(((bf16[256,384]{1,0:T(8,128)(2,1)}), bf16[4096,384]{1,0:T(8,128)(2,1)}) %all-gather.2.cloned.1.call-update) | async-done | bytes 3145744 | tf_op jit(solution)/shard_map/all_gather | solution.py:17
  53.2 4.3 %gather_fusion.1 = bf16[24,128,384]{2,1,0:T(8,128)(2,1)} fusion(bf16[32,128,384]{2,1,0:T(8,128)(2,1)} %bitcast.47, s32[1024]{0:T(1024)S(1)} %pad_clamp_fusion), kind=kCustom, calls=%fused_computation.1 | custom fusion | bytes 4718688 | tf_op jit(solution)/shard_map/jit(_take)/gather | solution.py:21
  57.5 2.0 broadcast_select_fusion
  59.5 0.0 copy-done
  59.5 1.5 fusion.22
  61.0 0.4 copy.9
  61.4 5.1 %tile.4 = bf16[2,16,256,384]{3,0,2,1:T(2,128)(2,1)S(1)} broadcast(bf16[2,256,384]{2,0,1:T(2,128)(2,1)S(1)} %copy.9), dimensions={0,2,3} | broadcast | bytes 6684672 | tf_op jit(solution)/shard_map/tile | solution.py:35
  66.5 143.9 %all_to_all.5 = bf16[2,4096,384]{2,0,1:T(2,128)(2,1)S(1)} all-to-all(bf16[2,4096,384]{2,0,1:T(2,128)(2,1)S(1)} %bitcast.46), channel_id=1, replica_groups=mesh['aux'=16,'occ'=16] {'occ'}, dimensions={1} | all-to-all | bytes 12582912 | tf_op jit(solution)/shard_map/all_to_all | solution.py:36
  210.4 3.8 %fusion.2 = f32[4096,256]{1,0:T(8,128)} fusion(bf16[2,256,384]{2,1,0:T(8,128)(2,1)S(1)} %bitcast.49, bf16[2,4096,384]{2,0,1:T(2,128)(2,1)S(1)} %all_to_all.5), kind=kOutput, calls=%fused_computation.4 | convolution fusion | flops 1610612736 | bytes 10878976 | tf_op jit(solution)/shard_map/pni,pmi->nm/dot_general | solution.py:8
  214.2 0.0 reduce-scatter.2.cloned.1.call-update
  214.2 80.9 %reduce-scatter.2.cloned.1.call-done = f32[256,256]{1,0:T(8,128)} async-done(((f32[4096,256]{1,0:T(8,128)}), f32[256,256]{1,0:T(8,128)}) %reduce-scatter.2.cloned.1.call-update) | async-done | bytes 262160 | tf_op jit(solution)/shard_map/reduce_scatter | solution.py:39
  (6 shorter events, 0.1 us)
Async XLA Ops:
  6.5 53.0 %copy-start = (bf16[2,24,128,128]{3,2,1,0:T(8,128)(2,1)S(1)}, bf16[2,24,128,128]{3,2,1,0:T(8,128)(2,1)}, u32[]{:S(2)}) copy-start(bf16[2,24,128,128]{3,2,1,0:T(8,128)(2,1)} %param.6) | copy-start | bytes 4718596
  6.5 46.6 %all-gather.2.cloned.1.call-start = ((), (), s32[]{:S(2)}) async-start(), calls=%async_computation.2 | async-start | bytes 3342336 | tf_op jit(solution)/shard_map/all_gather | solution.py:17
  7.3 287.8 %reduce-scatter.2.cloned.1.call-start = ((), (), s32[]{:S(2)}) async-start(), calls=%async_computation.3 | async-start | bytes 4456448 | tf_op jit(solution)/shard_map/reduce_scatter | solution.py:39
Sparse Core Ops, SparseCore 0:
  9.2 43.9 all-gather.1
  214.3 80.6 reduce-scatter.1
